TPU v7x, 32 devices: a whole 2x2x4 slice. The times are simulated.
32 devices in a mesh: gx: 4 (over y, core), gy: 4 (over z), gz: 2 (over x).
Axes of the slice: x: 2, y: 2, z: 4, core: 2. Of those that a mesh axis runs over, the one named last changes fastest.
Arguments:
- stiffness: float32 [32, 48, 256], P('gx', 'gy', 'gz'), may hold values from 0.5 to 5
- density: float32 [32, 48, 256], P('gx', 'gy', 'gz'), may hold values from 1 to 4
- load: float32 [3, 32, 48, 256], P(None, 'gx', 'gy', 'gz'), may hold values from -6 to 6
- alive: int32 [4, 32, 48, 256], P(None, 'gx', 'gy', 'gz'), may hold values 0 or 1
- surf_coords: float32 [512, 3, 128], P(('gx', 'gy', 'gz')), may hold values from 0 to 1
- surf_nodes: int32 [512, 128], P(('gx', 'gy', 'gz')), may hold values from 0 to 12287
- routes: int32 [4, 512], P(None, ('gx', 'gy', 'gz')), may hold values from 0 to 1, as said below
- pairs: int32 [4, 32, 64, 2], P(None, ('gx', 'gy', 'gz')), may hold values from 0 to 15, as said below
Outputs:
- element_velocity: float32 [3, 32, 48, 256], P(None, 'gx', 'gy', 'gz')
- element_stress: float32 [6, 32, 48, 256], P(None, 'gx', 'gy', 'gz')
Inputs may be any that keep to these rules, and one draw needn't show every extreme that they name: `routes`: in every step a device sends at most 8 of its blocks to one box, and all devices of a gz column send exactly 8 blocks to one common box of that column. `pairs`: every slot named is live at that box and step whenever the box holds a block at all.
All inputs are finite; a program needn't handle non-finite values. No bound on the sum of `alive` on one device may be relied on, other than what follows from the above.
Results may differ from a plain program's by a relative error of at most 0.0003.
Values sent between devices are 32-bit elements; how exact they have to be, the bound alone decides.
A program may use at most 64 MiB of HBM per device.

v0:
```python
import functools
import math

import jax
import jax.numpy as jnp
from jax import lax
from jax.experimental import pallas as pl
from jax.experimental.pallas import tpu as pltpu
from jax.sharding import PartitionSpec as P

REPULSION = 1.0
KERNEL_SCALE = 0.08
TIME_STEP = 0.2
HIGHEST = lax.Precision.HIGHEST
MESH = pl.DeviceIdType.MESH
F32 = jnp.float32
BF16 = jnp.bfloat16
STRETCH = math.sqrt(math.log2(math.e) / KERNEL_SCALE)


def iota(shape, dim):
    return lax.broadcasted_iota(jnp.int32, shape, dim)


def hdot(a, b):
    return jnp.dot(a, b, preferred_element_type=F32, precision=HIGHEST)


def split2(x):
    high = x.astype(BF16)
    return high, (x - high.astype(F32)).astype(BF16)


def sum_x(q):
    return jnp.concatenate([q[:1], q[:-1] + q[1:], q[-1:]], axis=0)


def diff_x(q):
    return jnp.concatenate([-q[:1], q[:-1] - q[1:], q[-1:]], axis=0)


def body(sizes, stiff_ref, dens_ref, load_ref, alive_ref, coords_ref, nodes_ref, routes_ref, pairt_ref, pair_ref,
         vout_ref, sout_ref, *scratch):
    (mod, big_f, rim_f, load_f, load_r, vel, vel_r, disp, disp_r, minv, minv_r, route_all, pos_all, slots, second,
     partial, send_f, ret, back_pick, rank_in, gather_w, lane_pick, scatter_w, scatter_l,
     x_send, x_recv, y_send, y_recv, z_send, z_recv,
     route_ss, route_rs, pos_ss, pos_rs, ret_ss, ret_rs, x_ss, x_rs, y_ss, y_rs, z_ss, z_rs) = scratch
    count_x, count_y, cx, cy, cz, sb, npair, steps, nz, cap = sizes
    nx = cx + 1
    rows = 16
    ix, iy, iz = lax.axis_index("gx"), lax.axis_index("gy"), lax.axis_index("gz")
    lanes = iota((rows, cz), 1)
    lane3 = iota((1, 1, cz), 2)

    def roll(v, shift, axis):
        return pltpu.roll(v, shift % v.shape[axis], axis)

    for ref in (x_send, x_recv, y_send, y_recv, z_send, z_recv, mod, slots, send_f):
        ref[...] = jnp.zeros(ref.shape, ref.dtype)

    sides = (("gx", ix, count_x), ("gy", iy, count_y), ("gz", iz, nz))
    barrier = pltpu.get_barrier_semaphore()
    expect = jnp.int32(nz - 1)
    for name, at, count in sides[:2]:
        @pl.when(at > 0)
        def _():
            pl.semaphore_signal(barrier, inc=1, device_id={name: at - 1}, device_id_type=MESH)

        @pl.when(at < count - 1)
        def _():
            pl.semaphore_signal(barrier, inc=1, device_id={name: at + 1}, device_id_type=MESH)
        expect = expect + jnp.where(at > 0, 1, 0) + jnp.where(at < count - 1, 1, 0)
    for other in range(1, nz):
        pl.semaphore_signal(barrier, inc=1, device_id={"gz": lax.rem(iz + other, nz)}, device_id_type=MESH)
    pl.semaphore_wait(barrier, expect)

    def column(send_ref, recv_ref, ss, rs):
        out = []
        for other in range(1, nz):
            to = lax.rem(iz + other, nz)
            out.append(pltpu.make_async_remote_copy(
                src_ref=send_ref(to), dst_ref=recv_ref, send_sem=ss.at[other - 1], recv_sem=rs.at[other - 1],
                device_id={"gz": to}, device_id_type=MESH))
        return out

    def pos_copies(phase):
        return column(lambda to: pos_all.at[phase, iz], pos_all.at[phase, iz], pos_ss.at[phase], pos_rs.at[phase])

    def ret_copies(t):
        return column(lambda to: send_f.at[t, to], ret.at[t, iz], ret_ss.at[t], ret_rs.at[t])

    route_copies = column(lambda to: route_all.at[iz], route_all.at[iz], route_ss, route_rs)

    route_all[iz] = jnp.full((8, 128), -1, jnp.int32)
    route_all[iz, 0:steps, 0:sb] = routes_ref[...]
    for x in range(3):
        pos_all[0, iz, :, x * 128:(x + 1) * 128] = coords_ref[:, x, :]
    for c in route_copies + pos_copies(0):
        c.start()

    for t in range(steps):
        mod[t, :, 0:cy, :] = stiff_ref[...] * alive_ref[t].astype(F32)
    for c in range(4):
        mod[steps + c, :, 0:cy, :] = 0.125 * (load_ref[c] if c < 3 else dens_ref[...])
    rim = jnp.zeros((rows, cz), F32)
    for c in range(4):
        q = sum_x(mod[steps + c])
        q = q + roll(q, 1, 1)
        r = roll(q, 1, 2)
        load_f[c] = q + jnp.where(lane3 > 0, r, 0.0)
        for i in range(nx):
            at = c * nx + i
            rim = rim + jnp.where(lanes == at, roll(r[i], at, 1), 0.0)
    load_r[...] = rim

    ids = nodes_ref[...]
    row = lax.shift_right_logical(ids, jnp.full(ids.shape, cz.bit_length() - 1, jnp.int32))
    lane = ids & (cz - 1)
    wide = row
    for m in range(1, cx):
        wide = wide + jnp.where(row >= cy * m, rows - cy, 0)
    depth = cx * rows
    wide_pad = jnp.concatenate([wide.astype(F32), jnp.zeros((128 - sb, 128), F32)], axis=0)
    wide_t = jnp.transpose(wide_pad)
    for s in range(sb):
        hot = (iota((depth, 128), 0) == wide[s:s + 1, :]).astype(F32).astype(BF16)
        gather_w[0:depth, s * 128:(s + 1) * 128] = hot
        gather_w[depth:2 * depth, s * 128:(s + 1) * 128] = hot
        lane_pick[s] = (iota((cz, 128), 0) == lane[s:s + 1, :]).astype(F32)
        col = jnp.broadcast_to(wide_t[:, s:s + 1], (128, depth))
        hot = (iota((128, depth), 1).astype(F32) == col).astype(F32).astype(BF16)
        scatter_w[s * 256:s * 256 + 128, :] = hot
        scatter_w[s * 256 + 128:s * 256 + 256, :] = hot

    def wait_all(copies):
        for c in copies:
            c.wait()

    wait_all(route_copies)
    upper = (iota((128, 128), 0) <= iota((128, 128), 1)).astype(F32)
    own = route_all[iz]
    for b in range(nz):
        hits = (route_all[b] == iz).astype(F32)
        rank_in[b] = jnp.where(hits > 0, jnp.dot(hits, upper, preferred_element_type=F32), 0.0)
    slot8 = nz * 8
    picks = []
    for b in range(nz):
        hits = (own == b).astype(F32)
        picks.append(jnp.where(hits > 0, jnp.dot(hits, upper, preferred_element_type=F32), 0.0))
    ranks8 = (iota((8, 128), 0) + 1).astype(F32)
    live8 = iota((8, 128), 0) < cap
    for t in range(steps):
        parts = [jnp.where((picks[b][t:t + 1, :] == ranks8) & live8, 1.0, 0.0) for b in range(nz)]
        table = jnp.concatenate(parts + [jnp.zeros((128 - slot8, 128), F32)], axis=0)
        back_pick[t] = jnp.transpose(table)[0:sb, :]

    def gather(phase):
        highs, lows = [], []
        for c in range(3):
            flat = jnp.transpose(disp[c, 0:cx].reshape(depth, cz))
            high, low = split2(flat)
            highs.append(high)
            lows.append(low)
        left = jnp.concatenate([jnp.concatenate(highs, axis=0), jnp.concatenate(lows, axis=0)], axis=1)
        for s in range(0, sb, 2):
            got = jnp.dot(left, gather_w[:, s * 128:(s + 2) * 128], preferred_element_type=F32)
            for h in range(2):
                for c in range(3):
                    part = got[c * cz:(c + 1) * cz, h * 128:(h + 1) * 128] * lane_pick[s + h]
                    pos_all[phase, iz, s + h:s + h + 1, c * 128:(c + 1) * 128] = (
                        jnp.sum(part, axis=0, keepdims=True) + coords_ref[s + h, c:c + 1, :])

    def build_slots(t, phase):
        live = []
        for b in range(nz):
            hot = jnp.where(rank_in[b, t:t + 1, :] == ranks8[0:cap], 1.0, 0.0)
            live.append(jnp.sum(hot, axis=1, keepdims=True))
            got = STRETCH * hdot(hot[:, 0:sb], pos_all[phase, b])
            for x in range(3):
                slots[x, b * cap:(b + 1) * cap, :] = got[:, x * 128:(x + 1) * 128]
        for x in range(3):
            flipped = jnp.transpose(slots[x])
            for k in range(nz * cap):
                second[k, x] = jnp.broadcast_to(flipped[:, k:k + 1], (128, 128))
        return live

    def pair_range(t, start, stop):
        def one(q, carry):
            p = pair_ref[t * npair * 2 + q * 2]
            r = pair_ref[t * npair * 2 + q * 2 + 1]
            xi = [jnp.broadcast_to(slots[x, pl.ds(p, 1), :], (8, 128)) for x in range(3)]
            acc = [jnp.zeros((8, 128), F32)] * 3
            for j in range(16):
                d = [xi[x] - second[r, x, j * 8:(j + 1) * 8, :] for x in range(3)]
                w = jnp.exp2(-(d[0] * d[0] + d[1] * d[1] + d[2] * d[2]))
                acc = [acc[x] + d[x] * w for x in range(3)]
            for x in range(3):
                partial[x, pl.ds(q, 1), :] = jnp.sum(acc[x], axis=0, keepdims=True)
            return carry
        lax.fori_loop(start, stop, one, 0)

    def finish_pairs(t, live):
        first = pairt_ref[t, 0:1, :]
        other = pairt_ref[t, 1:2, :]
        live_p = jnp.zeros((1, npair), F32)
        live_r = jnp.zeros((1, npair), F32)
        for b in range(nz):
            slot = iota((cap, npair), 0) + b * cap
            live_p = live_p + jnp.sum(jnp.where(first == slot, live[b], 0.0), axis=0, keepdims=True)
            live_r = live_r + jnp.sum(jnp.where(other == slot, live[b], 0.0), axis=0, keepdims=True)
        weight = live_p * live_r * (REPULSION / STRETCH)
        for b in range(nz):
            hot = jnp.where(first == iota((cap, npair), 0) + b * cap, weight, 0.0)
            for x in range(3):
                send_f[t, b, 0:cap, x * 128:(x + 1) * 128] = hdot(hot, partial[x])
        for c in ret_copies(t):
            c.start()
        ret[t, iz] = send_f[t, iz]

    def scatter(t):
        wait_all(ret_copies(t))
        force = hdot(back_pick[t, :, 0:slot8], ret[t].reshape(slot8, 384))
        for c in range(3):
            for s in range(sb):
                line = force[s:s + 1, c * 128:(c + 1) * 128]
                spread = lane_pick[s] * line
                high, low = split2(spread)
                scatter_l[c * cz:(c + 1) * cz, s * 256:s * 256 + 128] = high
                scatter_l[c * cz:(c + 1) * cz, s * 256 + 128:s * 256 + 256] = low
        total = jnp.dot(scatter_l[...], scatter_w[...], preferred_element_type=F32)
        for c in range(3):
            grid = jnp.transpose(total[c * cz:(c + 1) * cz, :]).reshape(cx, rows, cz)
            big_f[c, 0:cx] = big_f[c, 0:cx] + grid

    def corners(field, rim_value, c):
        u = field[c]
        edge = jnp.stack([roll(rim_value, -(c * nx + i), 1) for i in range(nx)])
        above = roll(jnp.where(lane3 == 0, edge, u), -1, 2)
        both = u + above
        step = above - u
        shifted = roll(both, -1, 1)
        return both + shifted, shifted - both, step + roll(step, -1, 1)

    def stress_of(modulus):
        grads = []
        rim_value = disp_r[...]
        for c in range(3):
            mean, along_y, along_z = corners(disp, rim_value, c)
            grads.append((0.25 * (mean[1:] - mean[:-1]), 0.25 * (along_y[1:] + along_y[:-1]),
                          0.25 * (along_z[1:] + along_z[:-1])))
        trace = grads[0][0] + grads[1][1] + grads[2][2]
        return (modulus * (2.0 * grads[0][0] + trace), modulus * (2.0 * grads[1][1] + trace),
                modulus * (2.0 * grads[2][2] + trace), modulus * (grads[0][1] + grads[1][0]),
                modulus * (grads[1][2] + grads[2][1]), modulus * (grads[0][2] + grads[2][0]))

    def internal(t):
        s = stress_of(mod[t])
        table = ((s[0], s[3], s[5]), (s[3], s[1], s[4]), (s[5], s[4], s[2]))
        rim = load_r[...]
        for c in range(3):
            a0 = -0.25 * diff_x(table[c][0])
            ay = -0.25 * sum_x(table[c][1])
            az = -0.25 * sum_x(table[c][2])
            a = (a0 - ay) + roll(a0 + ay, 1, 1)
            b = az + roll(az, 1, 1)
            r = roll(a + b, 1, 2)
            big_f[c] = load_f[c] + (a - b) + jnp.where(lane3 > 0, r, 0.0)
            for i in range(nx):
                at = c * nx + i
                rim = rim + jnp.where(lanes == at, roll(r[i], at, 1), 0.0)
        rim_f[...] = rim

    def axis_copies(side, send, recv, ss, rs, t, used):
        name, at, count = side
        out = []
        for way, to, sends, gets in ((0, at - 1, at > 0, at < count - 1), (1, at + 1, at < count - 1, at > 0)):
            out.append((pltpu.make_async_remote_copy(
                src_ref=send.at[t, way, 0:used], dst_ref=recv.at[t, way, 0:used], send_sem=ss.at[t, way],
                recv_sem=rs.at[t, way], device_id={name: to}, device_id_type=MESH), sends, gets))
        return out

    def start(copies):
        for copy, sends, _ in copies:
            @pl.when(sends)
            def _():
                copy.start()

    def finish(copies):
        for copy, sends, gets in copies:
            @pl.when(sends)
            def _():
                copy.wait_send()

            @pl.when(gets)
            def _():
                copy.wait_recv()

    def halo(t, fillers):
        comps = 4 if t == 0 else 3
        low_lane = functools.reduce(jnp.logical_or, [lanes == c * nx for c in range(4)])
        high_lane = functools.reduce(jnp.logical_or, [lanes == c * nx + cx for c in range(4)])
        for way, plane in ((0, 0), (1, cx)):
            x_send[t, way, 0] = rim_f[...]
            for c in range(comps):
                x_send[t, way, 1 + c] = big_f[c, plane]
        copies = axis_copies(sides[0], x_send, x_recv, x_ss, x_rs, t, comps + 1)
        start(copies)
        fillers[0]()
        finish(copies)
        for c in range(comps):
            big_f[c, 0] = big_f[c, 0] + x_recv[t, 1, 1 + c]
            big_f[c, cx] = big_f[c, cx] + x_recv[t, 0, 1 + c]
        rim_f[...] = (rim_f[...] + jnp.where(low_lane, roll(x_recv[t, 1, 0], -cx, 1), 0.0)
                      + jnp.where(high_lane, roll(x_recv[t, 0, 0], cx, 1), 0.0))

        used = -(-(1 + comps * nx) // 8) * 8
        for way, line in ((0, 0), (1, cy)):
            y_send[t, way, 0:1] = rim_f[line:line + 1]
            for c in range(comps):
                for i in range(nx):
                    at = 1 + c * nx + i
                    y_send[t, way, at:at + 1] = big_f[c, i, line:line + 1]
        copies = axis_copies(sides[1], y_send, y_recv, y_ss, y_rs, t, used)
        start(copies)
        fillers[1]()
        finish(copies)
        for way, line in ((1, 0), (0, cy)):
            rim_f[line:line + 1] = rim_f[line:line + 1] + y_recv[t, way, 0:1]
            for c in range(comps):
                for i in range(nx):
                    at = 1 + c * nx + i
                    big_f[c, i, line:line + 1] = big_f[c, i, line:line + 1] + y_recv[t, way, at:at + 1]

        packed = jnp.zeros((rows, cz), F32)
        for c in range(comps):
            for i in range(nx):
                at = c * nx + i
                packed = jnp.where(lanes == at, roll(big_f[c, i], at, 1), packed)
        z_send[t, 0] = packed
        z_send[t, 1] = rim_f[...]
        copies = axis_copies(sides[2], z_send, z_recv, z_ss, z_rs, t, rows)
        start(copies)
        fillers[2]()
        finish(copies)
        rim_f[...] = rim_f[...] + z_recv[t, 0]
        below = z_recv[t, 1]
        for c in range(comps):
            for i in range(nx):
                at = c * nx + i
                big_f[c, i] = big_f[c, i] + jnp.where(lanes == 0, roll(below, -at, 1), 0.0)

    def contact(t):
        cuts = [0, npair // 3, 2 * npair // 3, npair]
        return [lambda lo=lo, hi=hi: pair_range(t, lo, hi) for lo, hi in zip(cuts[:-1], cuts[1:])]

    nothing = [lambda: None] * 3

    wait_all(pos_copies(0))
    live = build_slots(0, 0)
    pair_range(0, 0, npair)
    finish_pairs(0, live)

    for t in range(steps):
        if t == 0:
            big_f[...] = load_f[...]
            rim_f[...] = load_r[...]
        else:
            if t + 1 < steps:
                gather(t)
                for c in pos_copies(t):
                    c.start()
            internal(t)
        scatter(t)
        if t + 1 < steps:
            if t > 0:
                wait_all(pos_copies(t))
            live = build_slots(t + 1, t)
            halo(t, contact(t + 1))
            finish_pairs(t + 1, live)
        else:
            halo(t, nothing)
        if t == 0:
            mass = big_f[3]
            minv[...] = jnp.where(mass > 0.0, 1.0 / mass, 0.0)
            held = jnp.where((lanes >= 3 * nx) & (lanes < 4 * nx), rim_f[...], 0.0)
            spread = roll(held, -3 * nx, 1) + roll(held, -2 * nx, 1) + roll(held, -nx, 1)
            minv_r[...] = jnp.where(spread > 0.0, 1.0 / spread, 0.0)
            for c in range(3):
                vel[c] = TIME_STEP * (big_f[c] * minv[...])
            vel_r[...] = TIME_STEP * (rim_f[...] * minv_r[...])
            disp[...] = TIME_STEP * vel[...]
            disp_r[...] = TIME_STEP * vel_r[...]
        else:
            for c in range(3):
                vel[c] = vel[c] + TIME_STEP * (big_f[c] * minv[...])
            vel_r[...] = vel_r[...] + TIME_STEP * (rim_f[...] * minv_r[...])
            disp[...] = disp[...] + TIME_STEP * vel[...]
            disp_r[...] = disp_r[...] + TIME_STEP * vel_r[...]

    rim_value = vel_r[...]
    for c in range(3):
        mean, _, _ = corners(vel, rim_value, c)
        vout_ref[c] = (0.125 * (mean[1:] + mean[:-1]))[:, 0:cy, :]
    s = stress_of(mod[steps - 1])
    for c in range(6):
        sout_ref[c] = s[c][:, 0:cy, :]


def per_device(stiffness, density, load, alive, surf_coords, surf_nodes, routes, pairs):
    cx, cy, cz = stiffness.shape
    steps = alive.shape[0]
    sb = surf_coords.shape[0]
    npair = pairs.shape[2]
    count_x, count_y, nz = (lax.axis_size(a) for a in ("gx", "gy", "gz"))
    cap = max(sb // 4, sb // nz)
    nx = cx + 1
    pairt = jnp.transpose(pairs[:, 0], (0, 2, 1))
    sizes = (count_x, count_y, cx, cy, cz, sb, npair, steps, nz, cap)
    vm = lambda *shape: pltpu.VMEM(shape, F32)
    dma = lambda *shape: pltpu.SemaphoreType.DMA(shape)
    column = max(nz - 1, 1)
    scratch = [
        vm(steps + 4, cx, 16, cz), vm(4, nx, 16, cz), vm(16, cz), vm(4, nx, 16, cz), vm(16, cz),
        vm(3, nx, 16, cz), vm(16, cz), vm(3, nx, 16, cz), vm(16, cz), vm(nx, 16, cz), vm(16, cz),
        pltpu.VMEM((nz, 8, 128), jnp.int32), vm(steps - 1, nz, sb, 384), vm(3, 128, 128), vm(nz * cap, 3, 128, 128),
        vm(3, npair, 128), vm(steps, nz, 8, 384), vm(steps, nz, 8, 384), vm(steps, sb, 128), vm(nz, 8, 128),
        pltpu.VMEM((2 * cx * 16, sb * 128), BF16), vm(sb, cz, 128), pltpu.VMEM((2 * sb * 128, cx * 16), BF16),
        pltpu.VMEM((3 * cz, 2 * sb * 128), BF16),
        vm(steps, 2, 5, 16, cz), vm(steps, 2, 5, 16, cz), vm(steps, 2, 40, cz), vm(steps, 2, 40, cz),
        vm(steps, 2, 16, cz), vm(steps, 2, 16, cz),
        dma(column), dma(column), dma(steps - 1, column), dma(steps - 1, column), dma(steps, column), dma(steps, column),
        dma(steps, 2), dma(steps, 2), dma(steps, 2), dma(steps, 2), dma(steps, 2), dma(steps, 2),
    ]
    vmem = pl.BlockSpec(memory_space=pltpu.VMEM)
    return pl.pallas_call(
        functools.partial(body, sizes),
        out_shape=(jax.ShapeDtypeStruct((3, cx, cy, cz), F32), jax.ShapeDtypeStruct((6, cx, cy, cz), F32)),
        in_specs=[vmem] * 8 + [pl.BlockSpec(memory_space=pltpu.SMEM)],
        out_specs=(vmem, vmem),
        scratch_shapes=scratch,
        compiler_params=pltpu.CompilerParams(collective_id=0, has_side_effects=True, vmem_limit_bytes=56 * 1024 * 1024),
    )(stiffness, density, load, alive, surf_coords, surf_nodes, routes, pairt, pairs.reshape(-1))


def solution(mesh):
    return jax.shard_map(
        per_device,
        mesh=mesh,
        in_specs=(
            P("gx", "gy", "gz"),
            P("gx", "gy", "gz"),
            P(None, "gx", "gy", "gz"),
            P(None, "gx", "gy", "gz"),
            P(("gx", "gy", "gz"), None, None),
            P(("gx", "gy", "gz"), None),
            P(None, ("gx", "gy", "gz")),
            P(None, ("gx", "gy", "gz"), None, None),
        ),
        out_specs=(P(None, "gx", "gy", "gz"), P(None, "gx", "gy", "gz")),
        check_vma=False,
    )
```

profile of v0, /device:TPU:1, one launch (start us, length us, event | category | flops | bytes accessed | tf_op | source)
XLA Modules:
  0.0 76.4 jit_solution(8497011638223832862)
XLA Ops:
  0.6 0.0 copy-start.2
  0.6 1.4 %copy.22.coords_ref = f32[16,3,128]{2,1,0:T(4,128)} copy(f32[16,3,128]{2,0,1:T(8,128)} %param.12) | data formatting | bytes 49152 | tf_op args[4]
  2.0 0.0 copy-done.2
  2.0 0.0 copy-start.3
  2.0 0.6 copy.18.stiff_ref
  2.6 0.2 copy-done.3
  2.8 0.0 copy-start.4
  2.8 0.6 copy.19.dens_ref
  3.4 0.1 copy-done.4
  3.5 0.0 copy-start.1
  3.5 0.1 copy.17
  3.6 0.7 reshape.7.pair_ref
  4.3 0.1 copy-done.1
  4.4 0.0 copy-start
  4.4 0.7 copy.20.load_ref
  5.1 0.3 copy-done
  5.4 0.7 copy.21.alive_ref
  6.1 66.8 %shard_map.95 = (f32[3,8,12,128]{3,2,1,0:T(8,128)}, f32[6,8,12,128]{3,2,1,0:T(8,128)}) custom-call(f32[8,12,128]{2,1,0:T(8,128)} %copy.18.stiff_ref, f32[8,12,128]{2,1,0:T(8,128)} %copy.19.dens_ref, f32[3,8,12,128]{3,2,1,0:T(8,128)} %copy.20.load_ref, s32[4,8,12,128]{3,2,1,0:T(8,128)} %copy.21.alive_ref, f32[16,3,128]{2,1,0:T(4,128)} %copy.22.coords_ref, ...), custom_call_target="tpu_custom_call" | custom-call | tf_op jit(solution)/shard_map/pallas_call | solution.py:435
  73.0 1.6 %copy.23 = f32[3,8,12,128]{3,1,2,0:T(8,128)} copy(f32[3,8,12,128]{3,2,1,0:T(8,128)} %get-tuple-element.4) | data formatting | bytes 294912 | tf_op jit(solution)/shard_map/pallas_call | solution.py:435
  74.6 1.8 %copy.24 = f32[6,8,12,128]{3,1,2,0:T(8,128)} copy(f32[6,8,12,128]{3,2,1,0:T(8,128)} %get-tuple-element.5) | data formatting | bytes 589824 | tf_op jit(solution)/shard_map/pallas_call | solution.py:435
Async XLA Ops:
  0.6 1.4 %copy-start.2 = (f32[8,12,128]{2,0,1:T(8,128)S(1)}, f32[8,12,128]{2,0,1:T(8,128)}, u32[]{:S(2)}) copy-start(f32[8,12,128]{2,0,1:T(8,128)} %param.8) | copy-start | bytes 147460
  2.0 0.8 %copy-start.3 = (f32[8,12,128]{2,0,1:T(8,128)S(1)}, f32[8,12,128]{2,0,1:T(8,128)}, u32[]{:S(2)}) copy-start(f32[8,12,128]{2,0,1:T(8,128)} %param.9) | copy-start | bytes 147460
  2.8 0.7 copy-start.4
  3.5 0.9 %copy-start.1 = (f32[3,8,12,128]{3,1,2,0:T(8,128)S(1)}, f32[3,8,12,128]{3,1,2,0:T(8,128)}, u32[]{:S(2)}) copy-start(f32[3,8,12,128]{3,1,2,0:T(8,128)} %param.10) | copy-start | bytes 442372
  4.4 1.0 %copy-start = (s32[4,8,12,128]{3,1,2,0:T(8,128)S(1)}, s32[4,8,12,128]{3,1,2,0:T(8,128)}, u32[]{:S(2)}) copy-start(s32[4,8,12,128]{3,1,2,0:T(8,128)} %param.11) | copy-start | bytes 589828
where the time goes:
time: 76.8 us; the launch traced here: 76.4 us
  Pallas kernels  66.8 us (87%)
  local copies, waits for them, and re-layouts  8.93 us (12%)
    pallas_call x1, Pallas kernels, per_device(): pl.pallas_call(functools.partial(body, sizes), out_shape=(jax.ShapeDtypeS...  66.8 us
    unnamed x16, local copies, waits for them, and re-layouts  4.77 us
    pallas_call x2, local copies, waits for them, and re-layouts, per_device(): pl.pallas_call(functools.partial(body, sizes), out_shape=(jax.ShapeDtypeS...  3.44 us

commit v1 on v0

--- a/solution.py
+++ b/solution.py
@@ -42,7 +42,7 @@
 def body(sizes, stiff_ref, dens_ref, load_ref, alive_ref, coords_ref, nodes_ref, routes_ref, pairt_ref, pair_ref,
          vout_ref, sout_ref, *scratch):
     (mod, big_f, rim_f, load_f, load_r, vel, vel_r, disp, disp_r, minv, minv_r, route_all, pos_all, slots, second,
-     partial, send_f, ret, back_pick, rank_in, gather_w, lane_pick, scatter_w, scatter_l,
+     partial, send_f, ret, back_pick, rank_in, gather_w, lane_pick, lane_pick_h, touch, scatter_w, scatter_l,
      x_send, x_recv, y_send, y_recv, z_send, z_recv,
      route_ss, route_rs, pos_ss, pos_rs, ret_ss, ret_rs, x_ss, x_rs, y_ss, y_rs, z_ss, z_rs) = scratch
     count_x, count_y, cx, cy, cz, sb, npair, steps, nz, cap = sizes
@@ -94,14 +94,16 @@
     route_all[iz] = jnp.full((8, 128), -1, jnp.int32)
     route_all[iz, 0:steps, 0:sb] = routes_ref[...]
     for x in range(3):
-        pos_all[0, iz, :, x * 128:(x + 1) * 128] = coords_ref[:, x, :]
+        pos_all[0, iz, :, x * 128:(x + 1) * 128] = coords_ref[x]
     for c in route_copies + pos_copies(0):
         c.start()
 
     for t in range(steps):
-        mod[t, :, 0:cy, :] = stiff_ref[...] * alive_ref[t].astype(F32)
+        for i in range(cx):
+            mod[t, i, 0:cy, :] = stiff_ref[:, i, :] * alive_ref[t, :, i, :].astype(F32)
     for c in range(4):
-        mod[steps + c, :, 0:cy, :] = 0.125 * (load_ref[c] if c < 3 else dens_ref[...])
+        for i in range(cx):
+            mod[steps + c, i, 0:cy, :] = 0.125 * (load_ref[c, :, i, :] if c < 3 else dens_ref[:, i, :])
     rim = jnp.zeros((rows, cz), F32)
     for c in range(4):
         q = sum_x(mod[steps + c])
@@ -124,9 +126,11 @@
     wide_t = jnp.transpose(wide_pad)
     for s in range(sb):
         hot = (iota((depth, 128), 0) == wide[s:s + 1, :]).astype(F32).astype(BF16)
-        gather_w[0:depth, s * 128:(s + 1) * 128] = hot
-        gather_w[depth:2 * depth, s * 128:(s + 1) * 128] = hot
-        lane_pick[s] = (iota((cz, 128), 0) == lane[s:s + 1, :]).astype(F32)
+        gather_w[s, 0:depth, :] = hot
+        gather_w[s, depth:2 * depth, :] = hot
+        pick = (iota((cz, 128), 0) == lane[s:s + 1, :]).astype(F32)
+        lane_pick[s] = pick
+        lane_pick_h[s] = pick.astype(BF16)
         col = jnp.broadcast_to(wide_t[:, s:s + 1], (128, depth))
         hot = (iota((128, depth), 1).astype(F32) == col).astype(F32).astype(BF16)
         scatter_w[s * 256:s * 256 + 128, :] = hot
@@ -163,12 +167,12 @@
             lows.append(low)
         left = jnp.concatenate([jnp.concatenate(highs, axis=0), jnp.concatenate(lows, axis=0)], axis=1)
         for s in range(0, sb, 2):
-            got = jnp.dot(left, gather_w[:, s * 128:(s + 2) * 128], preferred_element_type=F32)
+            got = jnp.dot(left, jnp.concatenate([gather_w[s], gather_w[s + 1]], axis=1), preferred_element_type=F32)
             for h in range(2):
                 for c in range(3):
                     part = got[c * cz:(c + 1) * cz, h * 128:(h + 1) * 128] * lane_pick[s + h]
                     pos_all[phase, iz, s + h:s + h + 1, c * 128:(c + 1) * 128] = (
-                        jnp.sum(part, axis=0, keepdims=True) + coords_ref[s + h, c:c + 1, :])
+                        jnp.sum(part, axis=0, keepdims=True) + coords_ref[c, s + h:s + h + 1, :])
 
     def build_slots(t, phase):
         live = []
@@ -184,10 +188,17 @@
                 second[k, x] = jnp.broadcast_to(flipped[:, k:k + 1], (128, 128))
         return live
 
+    unroll = 4
+
     def pair_range(t, start, stop):
-        def one(q, carry):
-            p = pair_ref[t * npair * 2 + q * 2]
-            r = pair_ref[t * npair * 2 + q * 2 + 1]
+        def some(at, carry):
+            for u in range(unroll):
+                one(start + at * unroll + u)
+            return carry
+
+        def one(q):
+            p = pair_ref[t, 0, q]
+            r = pair_ref[t, 1, q]
             xi = [jnp.broadcast_to(slots[x, pl.ds(p, 1), :], (8, 128)) for x in range(3)]
             acc = [jnp.zeros((8, 128), F32)] * 3
             for j in range(16):
@@ -196,8 +207,7 @@
                 acc = [acc[x] + d[x] * w for x in range(3)]
             for x in range(3):
                 partial[x, pl.ds(q, 1), :] = jnp.sum(acc[x], axis=0, keepdims=True)
-            return carry
-        lax.fori_loop(start, stop, one, 0)
+        lax.fori_loop(0, (stop - start) // unroll, some, 0)
 
     def finish_pairs(t, live):
         first = pairt_ref[t, 0:1, :]
@@ -222,15 +232,15 @@
         force = hdot(back_pick[t, :, 0:slot8], ret[t].reshape(slot8, 384))
         for c in range(3):
             for s in range(sb):
-                line = force[s:s + 1, c * 128:(c + 1) * 128]
-                spread = lane_pick[s] * line
-                high, low = split2(spread)
-                scatter_l[c * cz:(c + 1) * cz, s * 256:s * 256 + 128] = high
-                scatter_l[c * cz:(c + 1) * cz, s * 256 + 128:s * 256 + 256] = low
-        total = jnp.dot(scatter_l[...], scatter_w[...], preferred_element_type=F32)
+                line = jnp.broadcast_to(force[s:s + 1, c * 128:(c + 1) * 128], (16, 128))
+                for h, half in enumerate(split2(line)):
+                    spread = lane_pick_h[s].reshape(cz // 16, 16, 128) * half[None]
+                    scatter_l[2 * s + h, c * cz:(c + 1) * cz, :] = spread.reshape(cz, 128)
+        left = jnp.concatenate([scatter_l[k] for k in range(2 * sb)], axis=1)
+        total = jnp.dot(left, scatter_w[...], preferred_element_type=F32)
         for c in range(3):
             grid = jnp.transpose(total[c * cz:(c + 1) * cz, :]).reshape(cx, rows, cz)
-            big_f[c, 0:cx] = big_f[c, 0:cx] + grid
+            touch[c] = grid
 
     def corners(field, rim_value, c):
         u = field[c]
@@ -349,16 +359,25 @@
                 at = c * nx + i
                 big_f[c, i] = big_f[c, i] + jnp.where(lanes == 0, roll(below, -at, 1), 0.0)
 
-    def contact(t):
-        cuts = [0, npair // 3, 2 * npair // 3, npair]
-        return [lambda lo=lo, hi=hi: pair_range(t, lo, hi) for lo, hi in zip(cuts[:-1], cuts[1:])]
-
-    nothing = [lambda: None] * 3
+    def contact(t, phase):
+        cut = npair // 3 // unroll * unroll
+        held = []
+
+        def first():
+            if phase > 0:
+                wait_all(pos_copies(phase))
+            held.append(build_slots(t, phase))
+            pair_range(t, 0, cut)
+
+        def middle():
+            pair_range(t, cut, npair)
+            finish_pairs(t, held[0])
+
+        return [first, middle, lambda: scatter(t)]
 
     wait_all(pos_copies(0))
-    live = build_slots(0, 0)
-    pair_range(0, 0, npair)
-    finish_pairs(0, live)
+    for part in contact(0, 0):
+        part()
 
     for t in range(steps):
         if t == 0:
@@ -370,15 +389,9 @@
                 for c in pos_copies(t):
                     c.start()
             internal(t)
-        scatter(t)
-        if t + 1 < steps:
-            if t > 0:
-                wait_all(pos_copies(t))
-            live = build_slots(t + 1, t)
-            halo(t, contact(t + 1))
-            finish_pairs(t + 1, live)
-        else:
-            halo(t, nothing)
+        for c in range(3):
+            big_f[c, 0:cx] = big_f[c, 0:cx] + touch[c]
+        halo(t, contact(t + 1, t) if t + 1 < steps else [lambda: None] * 3)
         if t == 0:
             mass = big_f[3]
             minv[...] = jnp.where(mass > 0.0, 1.0 / mass, 0.0)
@@ -400,10 +413,13 @@
     rim_value = vel_r[...]
     for c in range(3):
         mean, _, _ = corners(vel, rim_value, c)
-        vout_ref[c] = (0.125 * (mean[1:] + mean[:-1]))[:, 0:cy, :]
+        mean = 0.125 * (mean[1:] + mean[:-1])
+        for i in range(cx):
+            vout_ref[c, :, i, :] = mean[i, 0:cy, :]
     s = stress_of(mod[steps - 1])
     for c in range(6):
-        sout_ref[c] = s[c][:, 0:cy, :]
+        for i in range(cx):
+            sout_ref[c, :, i, :] = s[c][i, 0:cy, :]
 
 
 def per_device(stiffness, density, load, alive, surf_coords, surf_nodes, routes, pairs):
@@ -424,22 +440,25 @@
         vm(3, nx, 16, cz), vm(16, cz), vm(3, nx, 16, cz), vm(16, cz), vm(nx, 16, cz), vm(16, cz),
         pltpu.VMEM((nz, 8, 128), jnp.int32), vm(steps - 1, nz, sb, 384), vm(3, 128, 128), vm(nz * cap, 3, 128, 128),
         vm(3, npair, 128), vm(steps, nz, 8, 384), vm(steps, nz, 8, 384), vm(steps, sb, 128), vm(nz, 8, 128),
-        pltpu.VMEM((2 * cx * 16, sb * 128), BF16), vm(sb, cz, 128), pltpu.VMEM((2 * sb * 128, cx * 16), BF16),
-        pltpu.VMEM((3 * cz, 2 * sb * 128), BF16),
+        pltpu.VMEM((sb, 2 * cx * 16, 128), BF16), vm(sb, cz, 128), pltpu.VMEM((sb, cz, 128), BF16),
+        vm(3, cx, 16, cz), pltpu.VMEM((2 * sb * 128, cx * 16), BF16),
+        pltpu.VMEM((2 * sb, 3 * cz, 128), BF16),
         vm(steps, 2, 5, 16, cz), vm(steps, 2, 5, 16, cz), vm(steps, 2, 40, cz), vm(steps, 2, 40, cz),
         vm(steps, 2, 16, cz), vm(steps, 2, 16, cz),
         dma(column), dma(column), dma(steps - 1, column), dma(steps - 1, column), dma(steps, column), dma(steps, column),
         dma(steps, 2), dma(steps, 2), dma(steps, 2), dma(steps, 2), dma(steps, 2), dma(steps, 2),
     ]
     vmem = pl.BlockSpec(memory_space=pltpu.VMEM)
-    return pl.pallas_call(
+    vel, stress = pl.pallas_call(
         functools.partial(body, sizes),
-        out_shape=(jax.ShapeDtypeStruct((3, cx, cy, cz), F32), jax.ShapeDtypeStruct((6, cx, cy, cz), F32)),
+        out_shape=(jax.ShapeDtypeStruct((3, cy, cx, cz), F32), jax.ShapeDtypeStruct((6, cy, cx, cz), F32)),
         in_specs=[vmem] * 8 + [pl.BlockSpec(memory_space=pltpu.SMEM)],
         out_specs=(vmem, vmem),
         scratch_shapes=scratch,
         compiler_params=pltpu.CompilerParams(collective_id=0, has_side_effects=True, vmem_limit_bytes=56 * 1024 * 1024),
-    )(stiffness, density, load, alive, surf_coords, surf_nodes, routes, pairt, pairs.reshape(-1))
+    )(jnp.swapaxes(stiffness, 0, 1), jnp.swapaxes(density, 0, 1), jnp.swapaxes(load, 1, 2), jnp.swapaxes(alive, 1, 2),
+      jnp.swapaxes(surf_coords, 0, 1), surf_nodes, routes, pairt, pairt)
+    return jnp.swapaxes(vel, 1, 2), jnp.swapaxes(stress, 1, 2)
 
 
 def solution(mesh):

time: 76.8 us -> 63.4 us (0.83)
  local copies, waits for them, and re-layouts: 8.93 us -> 2.34 us
  Pallas kernels: 66.8 us -> 60.3 us
    pallas_call x1, Pallas kernels: 66.8 us -> 60.3 us  [per_device(): pl.pallas_call(functools.partial(body, sizes), out_shape=(jax.ShapeDtypeS...]
    pallas_call x2 -> x0, local copies, waits for them, and re-layouts: 3.44 us -> none  [per_device(): pl.pallas_call(functools.partial(body, sizes), out_shape=(jax.ShapeDtypeS...]
    unnamed x16 -> x4, local copies, waits for them, and re-layouts: 4.77 us -> 2.34 us
where the time goes in v1:
time: 63.4 us; the launch traced here: 63.2 us
  Pallas kernels  60.3 us (95%)
  local copies, waits for them, and re-layouts  2.34 us (4%)
  between operations  0.65 us (1%)
    pallas_call x1, Pallas kernels, per_device(): pl.pallas_call(functools.partial(body, sizes), out_shape=(jax.ShapeDtypeS...  60.3 us
    unnamed x4, local copies, waits for them, and re-layouts  2.34 us

profile of v1, /device:TPU:1, one launch (start us, length us, event | category | flops | bytes accessed | tf_op | source)
XLA Modules:
  0.0 63.2 jit_solution(7692945831118829741)
XLA Ops:
  0.6 60.3 %shard_map.95 = (f32[3,12,8,128]{3,2,1,0:T(8,128)}, f32[6,12,8,128]{3,2,1,0:T(8,128)}) custom-call(f32[12,8,128]{2,1,0:T(8,128)} %bitcast.14, f32[12,8,128]{2,1,0:T(8,128)} %bitcast.15, f32[3,12,8,128]{3,2,1,0:T(8,128)} %bitcast.13, s32[4,12,8,128]{3,2,1,0:T(8,128)} %bitcast.11, f32[3,16,128]{2,1,0:T(8,128)} %bitcast.16, s32[16,128]{1,0:T(8,128)} %nodes_ref.1, ...), custom_call_target="tpu_custom_call" | custom-call | tf_op jit(solution)/shard_map/pallas_call | solution.py:452
  60.9 0.0 copy-start
  60.9 1.6 %copy.12 = f32[3,8,12,128]{3,1,2,0:T(8,128)} copy(f32[3,8,12,128]{3,1,2,0:T(8,128)} %bitcast.12) | data formatting | bytes 294912
  62.5 0.0 copy-done
  62.5 0.7 %copy.13 = f32[6,8,12,128]{3,1,2,0:T(8,128)} copy(f32[6,8,12,128]{3,1,2,0:T(8,128)S(1)} %bitcast.10) | data formatting | bytes 589824
Async XLA Ops:
  60.9 1.6 %copy-start = (f32[6,12,8,128]{3,2,1,0:T(8,128)S(1)}, f32[6,12,8,128]{3,2,1,0:T(8,128)}, u32[]{:S(2)}) copy-start(f32[6,12,8,128]{3,2,1,0:T(8,128)} %get-tuple-element.5) | copy-start | bytes 884740

commit v2 on v1

--- a/solution.py
+++ b/solution.py
@@ -39,9 +39,9 @@
     return jnp.concatenate([-q[:1], q[:-1] - q[1:], q[-1:]], axis=0)
 
 
-def body(sizes, stiff_ref, dens_ref, load_ref, alive_ref, coords_ref, nodes_ref, routes_ref, pairt_ref, pair_ref,
+def body(sizes, stiff_hbm, dens_hbm, load_hbm, alive_hbm, coords_ref, nodes_ref, routes_ref, pairt_ref, pair_ref,
          vout_ref, sout_ref, *scratch):
-    (mod, big_f, rim_f, load_f, load_r, vel, vel_r, disp, disp_r, minv, minv_r, route_all, pos_all, slots, second,
+    (stiff_ref, dens_ref, load_ref, alive_ref, in_sem, mod, big_f, rim_f, load_f, load_r, vel, vel_r, disp, disp_r, minv, minv_r, route_all, pos_all, slots, second,
      partial, send_f, ret, back_pick, rank_in, gather_w, lane_pick, lane_pick_h, touch, scatter_w, scatter_l,
      x_send, x_recv, y_send, y_recv, z_send, z_recv,
      route_ss, route_rs, pos_ss, pos_rs, ret_ss, ret_rs, x_ss, x_rs, y_ss, y_rs, z_ss, z_rs) = scratch
@@ -55,6 +55,11 @@
     def roll(v, shift, axis):
         return pltpu.roll(v, shift % v.shape[axis], axis)
 
+    inputs = [pltpu.make_async_copy(a, b, in_sem.at[k]) for k, (a, b) in enumerate((
+        (stiff_hbm, stiff_ref), (alive_hbm, alive_ref), (load_hbm, load_ref), (dens_hbm, dens_ref)))]
+    for c in inputs:
+        c.start()
+
     for ref in (x_send, x_recv, y_send, y_recv, z_send, z_recv, mod, slots, send_f):
         ref[...] = jnp.zeros(ref.shape, ref.dtype)
 
@@ -98,6 +103,8 @@
     for c in route_copies + pos_copies(0):
         c.start()
 
+    for c in inputs:
+        c.wait()
     for t in range(steps):
         for i in range(cx):
             mod[t, i, 0:cy, :] = stiff_ref[:, i, :] * alive_ref[t, :, i, :].astype(F32)
@@ -360,13 +367,15 @@
                 big_f[c, i] = big_f[c, i] + jnp.where(lanes == 0, roll(below, -at, 1), 0.0)
 
     def contact(t, phase):
-        cut = npair // 3 // unroll * unroll
+        cut = npair // (3 if phase > 0 else 2) // unroll * unroll
         held = []
 
         def first():
             if phase > 0:
                 wait_all(pos_copies(phase))
-            held.append(build_slots(t, phase))
+                held.append(build_slots(t, phase))
+            else:
+                held.append(early)
             pair_range(t, 0, cut)
 
         def middle():
@@ -376,8 +385,11 @@
         return [first, middle, lambda: scatter(t)]
 
     wait_all(pos_copies(0))
-    for part in contact(0, 0):
-        part()
+    live = build_slots(0, 0)
+    pair_range(0, 0, npair)
+    finish_pairs(0, live)
+    early = build_slots(1, 0)
+    scatter(0)
 
     for t in range(steps):
         if t == 0:
@@ -436,6 +448,7 @@
     dma = lambda *shape: pltpu.SemaphoreType.DMA(shape)
     column = max(nz - 1, 1)
     scratch = [
+        vm(cy, cx, cz), vm(cy, cx, cz), vm(3, cy, cx, cz), pltpu.VMEM((steps, cy, cx, cz), jnp.int32), dma(4),
         vm(steps + 4, cx, 16, cz), vm(4, nx, 16, cz), vm(16, cz), vm(4, nx, 16, cz), vm(16, cz),
         vm(3, nx, 16, cz), vm(16, cz), vm(3, nx, 16, cz), vm(16, cz), vm(nx, 16, cz), vm(16, cz),
         pltpu.VMEM((nz, 8, 128), jnp.int32), vm(steps - 1, nz, sb, 384), vm(3, 128, 128), vm(nz * cap, 3, 128, 128),
@@ -452,7 +465,7 @@
     vel, stress = pl.pallas_call(
         functools.partial(body, sizes),
         out_shape=(jax.ShapeDtypeStruct((3, cy, cx, cz), F32), jax.ShapeDtypeStruct((6, cy, cx, cz), F32)),
-        in_specs=[vmem] * 8 + [pl.BlockSpec(memory_space=pltpu.SMEM)],
+        in_specs=[pl.BlockSpec(memory_space=pltpu.MemorySpace.HBM)] * 4 + [vmem] * 4 + [pl.BlockSpec(memory_space=pltpu.SMEM)],
         out_specs=(vmem, vmem),
         scratch_shapes=scratch,
         compiler_params=pltpu.CompilerParams(collective_id=0, has_side_effects=True, vmem_limit_bytes=56 * 1024 * 1024),

time: 63.4 us -> 62.4 us (0.984)
  Pallas kernels: 60.3 us -> 59.1 us
    pallas_call x1, Pallas kernels: 60.3 us -> 59.1 us  [per_device(): pl.pallas_call(functools.partial(body, sizes), out_shape=(jax.ShapeDtypeS...]
where the time goes in v2:
time: 62.4 us; the launch traced here: 62.1 us
  Pallas kernels  59.1 us (95%)
  local copies, waits for them, and re-layouts  2.34 us (4%)
  between operations  0.65 us (1%)
    pallas_call x1, Pallas kernels, per_device(): pl.pallas_call(functools.partial(body, sizes), out_shape=(jax.ShapeDtypeS...  59.1 us
    unnamed x4, local copies, waits for them, and re-layouts  2.34 us

profile of v2, /device:TPU:1, one launch (start us, length us, event | category | flops | bytes accessed | tf_op | source)
XLA Modules:
  0.0 62.1 jit_solution(18136510381899425417)
XLA Ops:
  0.6 59.1 %shard_map.95 = (f32[3,12,8,128]{3,2,1,0:T(8,128)}, f32[6,12,8,128]{3,2,1,0:T(8,128)}) custom-call(f32[12,8,128]{2,1,0:T(8,128)} %bitcast.14, f32[12,8,128]{2,1,0:T(8,128)} %bitcast.15, f32[3,12,8,128]{3,2,1,0:T(8,128)} %bitcast.13, s32[4,12,8,128]{3,2,1,0:T(8,128)} %bitcast.11, f32[3,16,128]{2,1,0:T(8,128)} %bitcast.16, s32[16,128]{1,0:T(8,128)} %nodes_ref.1, ...), custom_call_target="tpu_custom_call" | custom-call | tf_op jit(solution)/shard_map/pallas_call | solution.py:465
  59.8 0.0 copy-start
  59.8 1.6 %copy.12 = f32[3,8,12,128]{3,1,2,0:T(8,128)} copy(f32[3,8,12,128]{3,1,2,0:T(8,128)} %bitcast.12) | data formatting | bytes 294912
  61.4 0.0 copy-done
  61.4 0.7 %copy.13 = f32[6,8,12,128]{3,1,2,0:T(8,128)} copy(f32[6,8,12,128]{3,1,2,0:T(8,128)S(1)} %bitcast.10) | data formatting | bytes 589824
Async XLA Ops:
  59.8 1.6 %copy-start = (f32[6,12,8,128]{3,2,1,0:T(8,128)S(1)}, f32[6,12,8,128]{3,2,1,0:T(8,128)}, u32[]{:S(2)}) copy-start(f32[6,12,8,128]{3,2,1,0:T(8,128)} %get-tuple-element.5) | copy-start | bytes 884740
